TPU v7x, 256 devices: a whole 4x4x8 slice. The times are simulated.
256 devices in a mesh: dp: 16 (over z_lo, x), tensor: 16 (over y, z_hi, core).
Axes of the slice: x: 4, y: 4, z: 8 (z_hi: 2, z_lo: 4; z = z_hi * 4 + z_lo), core: 2. Of those that a mesh axis runs over, the one named last changes fastest.
Arguments:
- out_grad: bfloat16 [2048, 5120], P('dp'), may hold values from -6 to 6
- gate_act: bfloat16 [2048, 25600], P('dp', 'tensor'), may hold values from -6 to 6
- up_act: bfloat16 [2048, 25600], P('dp', 'tensor'), may hold values from -6 to 6
- codes: int32 [5120, 25600], P('dp', 'tensor'), may hold values from 0 to 15
- zero_points: int32 [5120, 400], P('dp', 'tensor'), may hold values from 0 to 15
- scales: float32 [5120, 400], P('dp', 'tensor'), may hold values from 0.0009782797 to 0.003913119
- rotation: bfloat16 [1600, 1600], replicated, may hold values from -0.15625 to 0.15625
Outputs:
- grad_gate: bfloat16 [2048, 25600], P('dp', 'tensor')
- grad_up: bfloat16 [2048, 25600], P('dp', 'tensor')
- log_scale_grad: float32 [5120, 400], P('dp', 'tensor')
All inputs are finite; a program needn't handle non-finite values.
Results may differ from a plain program's by a relative error of at most 0.011.
Values may be sent and summed in bfloat16 or wider, within the bound.
A program may use at most 128 MiB of HBM per device.

v0:
```python
import math
import jax
import jax.numpy as jnp
from jax import lax
from jax.sharding import PartitionSpec as P


def sylvester(order_size):
    indices = jnp.arange(order_size, dtype=jnp.int32)
    common_bits = indices[:, None] & indices[None, :]
    parity = jnp.zeros((order_size, order_size), jnp.int32)
    for bit_number in range(order_size.bit_length()):
        parity = parity + (common_bits >> bit_number & 1)
    return (1 - 2 * (parity % 2)).astype(jnp.float32)


def spread(blocks, block_size):
    tok_rows = blocks.shape[0]
    local_blocks = blocks.shape[1] // block_size
    devices = lax.axis_size("tensor")
    norm_factor = 1.0 / math.sqrt(devices * local_blocks)
    hadamard = sylvester(devices * local_blocks).reshape(
        devices, local_blocks, devices, local_blocks
    )
    stacked = blocks.reshape(1, tok_rows, local_blocks, block_size)
    summed = jnp.einsum(
        "qtjc,qjpk->ptkc",
        lax.all_to_all(stacked, "tensor", split_axis=3, concat_axis=0, tiled=True).astype(
            jnp.float32
        ),
        hadamard,
        precision=lax.Precision.HIGHEST,
    )
    summed = (summed * norm_factor).astype(jnp.bfloat16)
    result = lax.all_to_all(summed, "tensor", split_axis=0, concat_axis=3, tiled=True)
    return result.reshape(tok_rows, local_blocks * block_size)


def on_device(out_grad, gate_act, up_act, codes, zero_points, scales, rotation):
    columns = gate_act.shape[1]
    block_size = rotation.shape[0]
    feat_rows = codes.shape[0]
    groups_here = scales.shape[1]
    group_cols = columns // groups_here
    gate32 = gate_act.astype(jnp.float32)
    up32 = up_act.astype(jnp.float32)
    sigmoid_gate = jax.nn.sigmoid(gate32)
    hidden = (gate32 * sigmoid_gate * up32).astype(jnp.bfloat16)
    mixed = jnp.dot(hidden, rotation, preferred_element_type=jnp.float32)
    mixed = mixed.astype(jnp.bfloat16)
    rotated = spread(mixed, block_size)
    levels = (codes.reshape(feat_rows, groups_here, group_cols) - zero_points[:, :, None]).astype(
        jnp.float32
    )
    weight = (levels * scales[:, :, None]).astype(jnp.bfloat16).reshape(feat_rows, columns)
    grad_slice = lax.all_to_all(out_grad, "dp", split_axis=1, concat_axis=0, tiled=True)
    weight_grad = lax.dot_general(
        grad_slice,
        lax.all_gather(rotated, "dp", axis=0, tiled=True),
        (((0,), (0,)), ((), ())),
        preferred_element_type=jnp.float32,
    )
    log_scale_grad = (
        jnp.sum(weight_grad.reshape(feat_rows, groups_here, group_cols) * levels, axis=2) * scales
    )
    grad_rotated = lax.psum_scatter(
        jnp.dot(grad_slice, weight, preferred_element_type=jnp.float32),
        "dp",
        scatter_dimension=0,
        tiled=True,
    )
    grad_mixed = spread(grad_rotated.astype(jnp.bfloat16), block_size)
    grad_hidden = lax.dot_general(
        grad_mixed, rotation, (((1,), (1,)), ((), ())), preferred_element_type=jnp.float32
    )
    grad_gate = (grad_hidden * up32 * sigmoid_gate * (1.0 + gate32 * (1.0 - sigmoid_gate))).astype(
        jnp.bfloat16
    )
    grad_up = (grad_hidden * gate32 * sigmoid_gate).astype(jnp.bfloat16)
    return (grad_gate, grad_up, log_scale_grad)


def solution(mesh):
    return jax.shard_map(
        on_device,
        mesh=mesh,
        in_specs=(
            P("dp", None),
            P("dp", "tensor"),
            P("dp", "tensor"),
            P("dp", "tensor"),
            P("dp", "tensor"),
            P("dp", "tensor"),
            P(),
        ),
        out_specs=(P("dp", "tensor"), P("dp", "tensor"), P("dp", "tensor")),
        check_vma=False,
    )
```

profile of v0, /device:TPU:90, one launch (start us, length us, event | category | flops | bytes accessed | tf_op | source)
XLA Modules:
  0.0 396.5 jit_solution(10725968039748546528)
XLA Ops:
  7.2 2.4 copy.24
  9.6 8.0 %all-to-all-start = ((bf16[128,16,320]{0,2,1:T(8,128)(2,1)}), bf16[128,16,320]{0,2,1:T(8,128)(2,1)}, u32[]{:S(2)}, u32[]{:S(2)}) async-start(bf16[128,16,320]{0,2,1:T(8,128)(2,1)} %bitcast.4), calls=%async_computation | async-start | bytes 2621440 | tf_op jit(solution)/shard_map/all_to_all | solution.py:56
  17.7 2.4 copy.23
  21.4 26.8 %all-to-all-done = bf16[128,16,320]{0,2,1:T(8,128)(2,1)} async-done(((bf16[128,16,320]{0,2,1:T(8,128)(2,1)}), bf16[128,16,320]{0,2,1:T(8,128)(2,1)}, u32[]{:S(2)}, u32[]{:S(2)}) %all-to-all-start) | async-done | bytes 1310752 | tf_op jit(solution)/shard_map/all_to_all | solution.py:56
  48.2 9.9 %convolution_bitcast_fusion = f32[2048,1600]{0,1:T(8,128)} fusion(bf16[320,1600]{0,1:T(8,128)(2,1)} %fusion, bf16[128,16,320]{0,2,1:T(8,128)(2,1)} %all-to-all-done), kind=kOutput, calls=%fused_computation | convolution fusion | flops 2097152000 | bytes 15441920 | tf_op jit(solution)/shard_map/dot_general | solution.py:67
  59.2 4.7 %fusion.2 = bf16[1,128,1,1600]{1,3,2,0:T(8,128)(2,1)S(1)} fusion(bf16[1600,1600]{1,0:T(8,128)(2,1)} %param.13, bf16[128,1600]{0,1:T(8,128)(2,1)S(1)} %copy-done.3, bf16[128,1600]{0,1:T(8,128)(2,1)S(1)} %copy-done.2), kind=kOutput, calls=%fused_computation.8 | convolution fusion | flops 657203200 | bytes 6348800 | tf_op jit(solution)/shard_map/dot_general | solution.py:49
  63.9 6.4 %copy.55 = bf16[1,128,1,1600]{1,2,0,3:T(2,128)(2,1)S(1)} copy(bf16[1,128,1,1600]{1,3,2,0:T(8,128)(2,1)S(1)} %fusion.2) | data formatting | bytes 819200 | tf_op jit(solution)/shard_map/reshape | solution.py:25
  70.8 9.9 %reduce.5 = bf16[1600,128]{1,0:T(8,128)(2,1)} reduce(bf16[1600,1,1,128]{3,2,1,0:T(2,128)(2,1)S(1)} %bitcast.84, bf16[]{:T(256)} %broadcast.409), dimensions={1,2}, to_apply=%bitcast.80.reduce_sub_computation | reduce | bytes 819202
  81.8 21.4 %all_to_all.79 = bf16[16,2,6400]{2,1,0:T(2,128)(2,1)} all-to-all(bf16[16,2,6400]{2,1,0:T(2,128)(2,1)S(1)} %reshape.191), channel_id=1, replica_groups=mesh['dp'=16,'tensor'=16] {'tensor'}, dimensions={0} | all-to-all | bytes 819200 | tf_op jit(solution)/shard_map/all_to_all | solution.py:28
  103.2 2.7 reshape.192
  106.0 7.6 %bitcast_reduce_fusion = bf16[128,1600]{0,1:T(8,128)(2,1)} fusion(bf16[1600,1,1,128]{3,2,1,0:T(2,128)(2,1)S(1)} %reshape.192), kind=kLoop, calls=%fused_computation.60 | loop fusion | bytes 819200 | tf_op jit(solution)/shard_map/all_to_all | solution.py:28
  115.3 18.8 %all_to_all.80 = bf16[16,128,1,100]{1,3,2,0:T(8,128)(2,1)S(1)} all-to-all(bf16[16,128,1,100]{1,3,2,0:T(8,128)(2,1)S(1)} %copy.31), channel_id=1, replica_groups=mesh['dp'=16,'tensor'=16] {'tensor'}, dimensions={0} | all-to-all | bytes 819200 | tf_op jit(solution)/shard_map/all_to_all | solution.py:35
  134.9 83.6 %reduce-scatter.2.cloned.1.call-done = f32[128,1600]{0,1:T(8,128)} async-done(((f32[2048,1600]{0,1:T(8,128)}), f32[128,1600]{0,1:T(8,128)}) %reduce-scatter.2.cloned.1.call-update) | async-done | bytes 819216 | tf_op jit(solution)/shard_map/reduce_scatter | solution.py:66
  219.8 6.4 %copy.56 = bf16[1,128,1,1600]{1,2,0,3:T(2,128)(2,1)S(1)} copy(bf16[1,128,1,1600]{1,3,2,0:T(8,128)(2,1)S(1)} %convert_bitcast_fusion) | data formatting | bytes 819200 | tf_op jit(solution)/shard_map/reshape | solution.py:25
  226.1 9.9 %reduce.4 = bf16[1600,128]{1,0:T(8,128)(2,1)} reduce(bf16[1600,1,1,128]{3,2,1,0:T(2,128)(2,1)S(1)} %bitcast.85, bf16[]{:T(256)} %broadcast.409), dimensions={1,2}, to_apply=%bitcast.81.reduce_sub_computation | reduce | bytes 819202
  237.1 20.5 %all_to_all.81 = bf16[16,2,6400]{2,1,0:T(2,128)(2,1)} all-to-all(bf16[16,2,6400]{2,1,0:T(2,128)(2,1)S(1)} %reshape.189), channel_id=1, replica_groups=mesh['dp'=16,'tensor'=16] {'tensor'}, dimensions={0} | all-to-all | bytes 819200 | tf_op jit(solution)/shard_map/all_to_all | solution.py:28
  257.7 2.7 reshape.190
  260.4 7.6 %bitcast_reduce_fusion.1 = bf16[128,1600]{0,1:T(8,128)(2,1)} fusion(bf16[1600,1,1,128]{3,2,1,0:T(2,128)(2,1)S(1)} %reshape.190), kind=kLoop, calls=%fused_computation.61 | loop fusion | bytes 819200 | tf_op jit(solution)/shard_map/all_to_all | solution.py:28
  270.5 5.8 %all-to-all-start.2 = ((bf16[16,128,1,100]{1,3,2,0:T(8,128)(2,1)}), bf16[16,128,1,100]{1,3,2,0:T(8,128)(2,1)S(1)}, u32[]{:S(2)}, u32[]{:S(2)}) async-start(bf16[16,128,1,100]{1,3,2,0:T(8,128)(2,1)} %copy.28), calls=%async_computation.3 | async-start | bytes 851968 | tf_op jit(solution)/shard_map/all_to_all | solution.py:35
  276.3 94.5 %all-gather.2.cloned.1.call-done = bf16[2048,1600]{0,1:T(8,128)(2,1)} async-done(((bf16[128,1600]{0,1:T(8,128)(2,1)}), bf16[2048,1600]{0,1:T(8,128)(2,1)}) %all-gather.2.cloned.1.call-update) | async-done | bytes 6553616 | tf_op jit(solution)/shard_map/all_gather | solution.py:59
  370.8 7.1 %convolution_bitcast_fusion.1 = f32[320,1600]{1,0:T(8,128)} fusion(bf16[2048,1600]{0,1:T(8,128)(2,1)} %all-gather.2.cloned.1.call-done, bf16[128,16,320]{0,2,1:T(8,128)(2,1)} %all-to-all-done), kind=kOutput, calls=%fused_computation.1 | convolution fusion | flops 2097152000 | bytes 9912320 | tf_op jit(solution)/shard_map/dot_general | solution.py:57
  377.9 3.1 copy.32
  381.0 2.3 multiply_reduce_fusion
  384.0 5.3 %fusion.20 = (bf16[128,1600]{0,1:T(8,128)(2,1)}, bf16[128,1600]{0,1:T(8,128)(2,1)}) fusion(bf16[128,1600]{0,1:T(8,128)(2,1)} %param.8, bf16[128,1600]{0,1:T(8,128)(2,1)} %param.9, bf16[1600,1600]{1,0:T(8,128)(2,1)} %param.13, bf16[128,1600]{0,1:T(8,128)(2,1)S(1)} %reshape.180), kind=kOutput, calls=%fused_computation.34 | convolution fusion | flops 658432000 | bytes 7168000 | tf_op jit(solution)/shard_map/dot_general | solution.py:73
  (27 shorter events, 12.1 us)
Async XLA Ops:
  9.6 38.6 %all-to-all-start = ((bf16[128,16,320]{0,2,1:T(8,128)(2,1)}), bf16[128,16,320]{0,2,1:T(8,128)(2,1)}, u32[]{:S(2)}, u32[]{:S(2)}) async-start(bf16[128,16,320]{0,2,1:T(8,128)(2,1)} %bitcast.4), calls=%async_computation | async-start | bytes 2621440 | tf_op jit(solution)/shard_map/all_to_all | solution.py:56
  17.6 2.4 copy-start
  17.6 2.4 copy-start.1
  17.6 200.9 %reduce-scatter.2.cloned.1.call-start = ((), (), s32[]{:S(2)}) async-start(), calls=%async_computation.6 | async-start | bytes 13926400 | tf_op jit(solution)/shard_map/reduce_scatter | solution.py:66
  58.1 1.0 copy-start.2
  58.1 1.1 copy-start.3
  58.1 312.7 %all-gather.2.cloned.1.call-start = ((), (), s32[]{:S(2)}) async-start(), calls=%async_computation.7 | async-start | bytes 6963200 | tf_op jit(solution)/shard_map/all_gather | solution.py:59
  270.5 113.5 %all-to-all-start.2 = ((bf16[16,128,1,100]{1,3,2,0:T(8,128)(2,1)}), bf16[16,128,1,100]{1,3,2,0:T(8,128)(2,1)S(1)}, u32[]{:S(2)}, u32[]{:S(2)}) async-start(bf16[16,128,1,100]{1,3,2,0:T(8,128)(2,1)} %copy.28), calls=%async_computation.3 | async-start | bytes 851968 | tf_op jit(solution)/shard_map/all_to_all | solution.py:35
Sparse Core Ops, SparseCore 0:
  58.3 160.2 reduce-scatter.1
  220.9 149.8 all-gather.1
where the time goes:
time: 401 us; the launch traced here: 396 us
  waiting for transfers between devices  205 us (51%)
  blocking collectives  60.8 us (15%)
  local copies, waits for them, and re-layouts  48.7 us (12%)
  matrix products  28 us (7%)
  other arithmetic  25.3 us (6%)
  starting transfers between devices  14.4 us (4%)
  between operations  14.4 us (4%)
    all_gather x1, waiting for transfers between devices, on_device(): lax.all_gather(rotated, 'dp', axis=0, tiled=True)  94.5 us
    reduce_scatter x1, waiting for transfers between devices, on_device(): lax.psum_scatter(jnp.dot(grad_slice, weight, preferred_element_type=jnp.f...  83.6 us
    all_to_all x2, blocking collectives, spread(): lax.all_to_all(stacked, 'tensor', split_axis=3, concat_axis=0, tiled=True)  41.9 us
    all_to_all x1, waiting for transfers between devices, on_device(): lax.all_to_all(out_grad, 'dp', split_axis=1, concat_axis=0, tiled=True)  26.8 us
    unnamed x2, other arithmetic  19.8 us
    all_to_all x1, blocking collectives, spread(): lax.all_to_all(summed, 'tensor', split_axis=0, concat_axis=3, tiled=True)  18.8 us
    all_to_all x4, local copies, waits for them, and re-layouts, spread(): lax.all_to_all(stacked, 'tensor', split_axis=3, concat_axis=0, tiled=True)  17.3 us
    unnamed x15, local copies, waits for them, and re-layouts  13.6 us
  transfers between devices with their start and end apart: 4, of which 3 were waited for; matrix products, arithmetic and copies ran while one was open for 21% of the time, Pallas kernels for 0%

commit v1 on v0

--- a/solution.py
+++ b/solution.py
@@ -56,7 +56,15 @@
     grad_slice = lax.all_to_all(out_grad, "dp", split_axis=1, concat_axis=0, tiled=True)
     weight_grad = lax.dot_general(
         grad_slice,
-        lax.all_gather(rotated, "dp", axis=0, tiled=True),
+        jnp.concatenate(
+            lax.all_to_all(
+                jnp.stack([rotated] * lax.psum(1, axis_name="dp")),
+                axis_name="dp",
+                split_axis=0,
+                concat_axis=0,
+            ),
+            axis=0,
+        ),
         (((0,), (0,)), ((), ())),
         preferred_element_type=jnp.float32,
     )

time: 401 us -> 479 us (1.19)
  the two profiles are of different devices: /device:TPU:90 before, /device:TPU:193 now
where the time goes in v1:
time: 479 us; the launch traced here: 470 us
  waiting for transfers between devices  170 us (35%)
  blocking collectives  136 us (28%)
  local copies, waits for them, and re-layouts  54.9 us (11%)
  starting transfers between devices  41 us (9%)
  matrix products  28.1 us (6%)
  other arithmetic  25.7 us (5%)
  between operations  14.4 us (3%)
    all_to_all x1, blocking collectives, spread(): lax.all_to_all(stacked, 'tensor', split_axis=3, concat_axis=0, tiled=True)  136 us
    all_to_all x1, waiting for transfers between devices, on_device(): lax.all_to_all(jnp.stack([rotated] * lax.psum(1, axis_name='dp')), axis_n...  135 us
    all_to_all x1, waiting for transfers between devices, on_device(): lax.all_to_all(out_grad, 'dp', split_axis=1, concat_axis=0, tiled=True)  27.2 us
    unnamed x2, other arithmetic  20.3 us
    all_to_all x2, starting transfers between devices, spread(): lax.all_to_all(summed, 'tensor', split_axis=0, concat_axis=3, tiled=True)  19.5 us
    all_to_all x4, local copies, waits for them, and re-layouts, spread(): lax.all_to_all(stacked, 'tensor', split_axis=3, concat_axis=0, tiled=True)  17.3 us
    unnamed x17, local copies, waits for them, and re-layouts  14.9 us
    reshape x2, local copies, waits for them, and re-layouts, spread(): stacked = blocks.reshape(1, tok_rows, local_blocks, block_size)  12.7 us
  transfers between devices with their start and end apart: 6, of which 3 were waited for; matrix products, arithmetic and copies ran while one was open for 18% of the time, Pallas kernels for 0%

profile of v1, /device:TPU:193, one launch (start us, length us, event | category | flops | bytes accessed | tf_op | source)
XLA Modules:
  0.0 470.3 jit_solution(4171967760841722243)
XLA Ops:
  7.2 2.4 copy.25
  9.6 6.6 %all-to-all-start = ((bf16[128,16,320]{0,2,1:T(8,128)(2,1)}), bf16[128,16,320]{0,2,1:T(8,128)(2,1)}, u32[]{:S(2)}, u32[]{:S(2)}) async-start(bf16[128,16,320]{0,2,1:T(8,128)(2,1)} %bitcast.4), calls=%async_computation | async-start | bytes 2621440 | tf_op jit(solution)/shard_map/all_to_all | solution.py:56
  20.0 27.2 %all-to-all-done = bf16[128,16,320]{0,2,1:T(8,128)(2,1)} async-done(((bf16[128,16,320]{0,2,1:T(8,128)(2,1)}), bf16[128,16,320]{0,2,1:T(8,128)(2,1)}, u32[]{:S(2)}, u32[]{:S(2)}) %all-to-all-start) | async-done | bytes 1310752 | tf_op jit(solution)/shard_map/all_to_all | solution.py:56
  47.2 9.9 %convolution_bitcast_fusion = f32[2048,1600]{0,1:T(8,128)} fusion(bf16[320,1600]{0,1:T(8,128)(2,1)} %fusion, bf16[128,16,320]{0,2,1:T(8,128)(2,1)} %all-to-all-done), kind=kOutput, calls=%fused_computation | convolution fusion | flops 2097152000 | bytes 15441920 | tf_op jit(solution)/shard_map/dot_general | solution.py:75
  58.2 4.7 %fusion.2 = bf16[1,128,1,1600]{1,3,2,0:T(8,128)(2,1)S(1)} fusion(bf16[1600,1600]{1,0:T(8,128)(2,1)} %param.13, bf16[128,1600]{0,1:T(8,128)(2,1)S(1)} %copy-done.4, bf16[128,1600]{0,1:T(8,128)(2,1)S(1)} %copy-done.3), kind=kOutput, calls=%fused_computation.8 | convolution fusion | flops 657203200 | bytes 6348800 | tf_op jit(solution)/shard_map/dot_general | solution.py:49
  62.9 6.4 %copy.52 = bf16[1,128,1,1600]{1,2,0,3:T(2,128)(2,1)S(1)} copy(bf16[1,128,1,1600]{1,3,2,0:T(8,128)(2,1)S(1)} %fusion.2) | data formatting | bytes 819200 | tf_op jit(solution)/shard_map/reshape | solution.py:25
  69.8 10.4 %reduce.5 = bf16[1600,128]{1,0:T(8,128)(2,1)} reduce(bf16[1600,1,1,128]{3,2,1,0:T(2,128)(2,1)S(1)} %bitcast.83, bf16[]{:T(256)} %broadcast.410), dimensions={1,2}, to_apply=%bitcast.79.reduce_sub_computation | reduce | bytes 819202
  81.3 136.3 %all_to_all.84 = bf16[16,2,6400]{2,1,0:T(2,128)(2,1)} all-to-all(bf16[16,2,6400]{2,1,0:T(2,128)(2,1)S(1)} %reshape.191), channel_id=1, replica_groups=mesh['dp'=16,'tensor'=16] {'tensor'}, dimensions={0} | all-to-all | bytes 819200 | tf_op jit(solution)/shard_map/all_to_all | solution.py:28
  217.6 2.7 reshape.192
  220.3 7.6 %bitcast_reduce_fusion = bf16[128,1600]{0,1:T(8,128)(2,1)} fusion(bf16[1600,1,1,128]{3,2,1,0:T(2,128)(2,1)S(1)} %reshape.192), kind=kLoop, calls=%fused_computation.59 | loop fusion | bytes 819200 | tf_op jit(solution)/shard_map/all_to_all | solution.py:28
  230.4 10.6 %all-to-all-start.4 = ((bf16[16,128,1,100]{1,3,2,0:T(8,128)(2,1)}), bf16[16,128,1,100]{1,3,2,0:T(8,128)(2,1)}, u32[]{:S(2)}, u32[]{:S(2)}) async-start(bf16[16,128,1,100]{1,3,2,0:T(8,128)(2,1)} %copy.32), calls=%async_computation.5 | async-start | bytes 851968 | tf_op jit(solution)/shard_map/all_to_all | solution.py:35
  242.2 6.4 %copy.53 = bf16[1,128,1,1600]{1,2,0,3:T(2,128)(2,1)S(1)} copy(bf16[1,128,1,1600]{1,3,2,0:T(8,128)(2,1)S(1)} %convert_bitcast_fusion) | data formatting | bytes 819200 | tf_op jit(solution)/shard_map/reshape | solution.py:25
  248.6 9.9 %reduce.4 = bf16[1600,128]{1,0:T(8,128)(2,1)} reduce(bf16[1600,1,1,128]{3,2,1,0:T(2,128)(2,1)S(1)} %bitcast.84, bf16[]{:T(256)} %broadcast.410), dimensions={1,2}, to_apply=%bitcast.80.reduce_sub_computation | reduce | bytes 819202
  260.4 9.7 %all-to-all-start.1 = ((bf16[16,2,6400]{2,1,0:T(2,128)(2,1)}), bf16[16,2,6400]{2,1,0:T(2,128)(2,1)S(1)}, u32[]{:S(2)}, u32[]{:S(2)}) async-start(bf16[16,2,6400]{2,1,0:T(2,128)(2,1)} %reshape.189), calls=%async_computation.2 | async-start | bytes 819200 | tf_op jit(solution)/shard_map/all_to_all | solution.py:28
  271.1 7.4 %all-to-all-done.1 = bf16[16,2,6400]{2,1,0:T(2,128)(2,1)S(1)} async-done(((bf16[16,2,6400]{2,1,0:T(2,128)(2,1)}), bf16[16,2,6400]{2,1,0:T(2,128)(2,1)S(1)}, u32[]{:S(2)}, u32[]{:S(2)}) %all-to-all-start.1) | async-done | bytes 409632 | tf_op jit(solution)/shard_map/all_to_all | solution.py:28
  278.5 4.0 stack.3
  282.5 5.2 %all-to-all-start.5 = ((bf16[16,128,1600]{1,2,0:T(8,128)(2,1)}), bf16[16,128,1600]{1,2,0:T(8,128)(2,1)}, u32[]{:S(2)}, u32[]{:S(2)}) async-start(bf16[16,128,1600]{1,2,0:T(8,128)(2,1)} %stack.3), calls=%async_computation.6 | async-start | bytes 13107200 | tf_op jit(solution)/shard_map/all_to_all | solution.py:60
  287.7 2.7 reshape.190
  290.4 7.6 %bitcast_reduce_fusion.1 = bf16[128,1600]{0,1:T(8,128)(2,1)} fusion(bf16[1600,1,1,128]{3,2,1,0:T(2,128)(2,1)S(1)} %reshape.190), kind=kLoop, calls=%fused_computation.60 | loop fusion | bytes 819200 | tf_op jit(solution)/shard_map/all_to_all | solution.py:28
  300.5 135.2 %all-to-all-done.5 = bf16[16,128,1600]{1,2,0:T(8,128)(2,1)} async-done(((bf16[16,128,1600]{1,2,0:T(8,128)(2,1)}), bf16[16,128,1600]{1,2,0:T(8,128)(2,1)}, u32[]{:S(2)}, u32[]{:S(2)}) %all-to-all-start.5) | async-done | bytes 6553632 | tf_op jit(solution)/shard_map/all_to_all | solution.py:60
  435.6 8.9 %all-to-all-start.2 = ((bf16[16,128,1,100]{1,3,2,0:T(8,128)(2,1)}), bf16[16,128,1,100]{1,3,2,0:T(8,128)(2,1)S(1)}, u32[]{:S(2)}, u32[]{:S(2)}) async-start(bf16[16,128,1,100]{1,3,2,0:T(8,128)(2,1)} %copy.29), calls=%async_computation.3 | async-start | bytes 851968 | tf_op jit(solution)/shard_map/all_to_all | solution.py:35
  444.5 7.1 %convolution_bitcast_fusion.1 = f32[320,1600]{1,0:T(8,128)} fusion(bf16[16,128,1600]{1,2,0:T(8,128)(2,1)} %all-to-all-done.5, bf16[128,16,320]{0,2,1:T(8,128)(2,1)} %all-to-all-done), kind=kOutput, calls=%fused_computation.1 | convolution fusion | flops 2097152000 | bytes 9912320 | tf_op jit(solution)/shard_map/dot_general | solution.py:57
  451.7 3.1 copy.33
  457.8 5.3 %fusion.19 = (bf16[128,1600]{0,1:T(8,128)(2,1)}, bf16[128,1600]{0,1:T(8,128)(2,1)}) fusion(bf16[128,1600]{0,1:T(8,128)(2,1)} %param.8, bf16[128,1600]{0,1:T(8,128)(2,1)} %param.9, bf16[1600,1600]{1,0:T(8,128)(2,1)} %param.13, bf16[128,1600]{0,1:T(8,128)(2,1)S(1)} %reshape.180), kind=kOutput, calls=%fused_computation.33 | convolution fusion | flops 658432000 | bytes 7168000 | tf_op jit(solution)/shard_map/dot_general | solution.py:81
  (31 shorter events, 18.5 us)
Async XLA Ops:
  9.6 37.6 %all-to-all-start = ((bf16[128,16,320]{0,2,1:T(8,128)(2,1)}), bf16[128,16,320]{0,2,1:T(8,128)(2,1)}, u32[]{:S(2)}, u32[]{:S(2)}) async-start(bf16[128,16,320]{0,2,1:T(8,128)(2,1)} %bitcast.4), calls=%async_computation | async-start | bytes 2621440 | tf_op jit(solution)/shard_map/all_to_all | solution.py:56
  16.2 2.4 copy-start.1
  16.2 2.4 copy-start.2
  16.2 224.8 %reduce-scatter.2.cloned.1.call-start = ((), (), s32[]{:S(2)}) async-start(), calls=%async_computation.7 | async-start | bytes 13926400 | tf_op jit(solution)/shard_map/reduce_scatter | solution.py:74
  57.1 1.0 copy-start.3
  57.1 1.1 copy-start.4
  230.4 30.0 %all-to-all-start.4 = ((bf16[16,128,1,100]{1,3,2,0:T(8,128)(2,1)}), bf16[16,128,1,100]{1,3,2,0:T(8,128)(2,1)}, u32[]{:S(2)}, u32[]{:S(2)}) async-start(bf16[16,128,1,100]{1,3,2,0:T(8,128)(2,1)} %copy.32), calls=%async_computation.5 | async-start | bytes 851968 | tf_op jit(solution)/shard_map/all_to_all | solution.py:35
  260.4 18.2 %all-to-all-start.1 = ((bf16[16,2,6400]{2,1,0:T(2,128)(2,1)}), bf16[16,2,6400]{2,1,0:T(2,128)(2,1)S(1)}, u32[]{:S(2)}, u32[]{:S(2)}) async-start(bf16[16,2,6400]{2,1,0:T(2,128)(2,1)} %reshape.189), calls=%async_computation.2 | async-start | bytes 819200 | tf_op jit(solution)/shard_map/all_to_all | solution.py:28
  278.5 4.0 copy-start
  282.5 153.1 %all-to-all-start.5 = ((bf16[16,128,1600]{1,2,0:T(8,128)(2,1)}), bf16[16,128,1600]{1,2,0:T(8,128)(2,1)}, u32[]{:S(2)}, u32[]{:S(2)}) async-start(bf16[16,128,1600]{1,2,0:T(8,128)(2,1)} %stack.3), calls=%async_computation.6 | async-start | bytes 13107200 | tf_op jit(solution)/shard_map/all_to_all | solution.py:60
  435.6 22.1 %all-to-all-start.2 = ((bf16[16,128,1,100]{1,3,2,0:T(8,128)(2,1)}), bf16[16,128,1,100]{1,3,2,0:T(8,128)(2,1)S(1)}, u32[]{:S(2)}, u32[]{:S(2)}) async-start(bf16[16,128,1,100]{1,3,2,0:T(8,128)(2,1)} %copy.29), calls=%async_computation.3 | async-start | bytes 851968 | tf_op jit(solution)/shard_map/all_to_all | solution.py:35
Sparse Core Ops, SparseCore 0:
  57.2 165.9 reduce-scatter.1
